TPU v7x, 256 devices: a whole 4x4x8 slice. The times are simulated.
256 devices in a mesh: pw: 64 (over x_lo, z, y), band: 4 (over x_hi, core).
Axes of the slice: x: 4 (x_hi: 2, x_lo: 2; x = x_hi * 2 + x_lo), y: 4, z: 8, core: 2. Of those that a mesh axis runs over, the one named last changes fastest.
Arguments:
- residual_directions: float32 [2, 512, 4, 16384], P(None, 'pw', 'band'), may hold values from -6 to 6
- local_field_applied: float32 [2, 512, 4, 16384], P(None, 'pw', 'band'), may hold values from -6 to 6
- orbital_running_sum: bfloat16 [2, 2048, 4, 16384], P(None, None, 'band', 'pw'), may hold values from -6 to 6
- energy_operator_running_sum: bfloat16 [2, 2048, 4, 16384], P(None, None, 'band', 'pw'), may hold values from -6 to 6
- coefficient_store: bfloat16 [4, 512, 2048], P('band'), may hold values from -0.25 to 0.25
- slab_keepers: int32 [2], replicated, may hold values from 0 to 3
- lattice_position: int32 [4, 16384], P('band', 'pw'), may hold values from 0 to 262143
Outputs:
- psi_new: bfloat16 [2, 2048, 4, 16384], P(None, None, 'band', 'pw')
- hpsi_new: bfloat16 [2, 2048, 4, 16384], P(None, None, 'band', 'pw')
Inputs may be any that keep to these rules, and one draw needn't show every extreme that they name: `slab_keepers`: each panel's owner is an index along band. `lattice_position`: grid points are row-major indices of a 64 x 64 x 64 grid, not necessarily distinct.
All inputs are finite; a program needn't handle non-finite values.
Results may differ from a plain program's by a relative error of at most 0.001.
Values may be sent and summed in bfloat16 or wider, within the bound.
No kernel may reach another device: no remote copies, remote signals or barrier semaphores. Data moves between devices by JAX's collectives and lax.ppermute only.
A program may use at most 128 MiB of HBM per device.

v0:
```python
import jax
import jax.numpy as jnp
from jax import lax
from jax.sharding import PartitionSpec as P

RESIDUAL_NUMBER = 512
SLAB_LENGTH = 256
GRID = 64


def from_root(value, axis, source):
    kept = jnp.where(lax.axis_index(axis) == source, value, 0).astype(value.dtype)
    return lax.psum(kept, axis)


def kinetic_of(lattice_position):
    first = lattice_position // (GRID * GRID)
    second = lattice_position // GRID % GRID
    third = lattice_position % GRID
    total = jnp.zeros(lattice_position.shape, jnp.int32)
    for index in (first, second, third):
        folded = jnp.where(index >= GRID // 2, index - GRID, index)
        total = total + folded * folded
    return total.astype(jnp.float32) / (GRID * GRID)


def rotate_plane(panels, plane):
    total = None
    for subspace_slab in range(len(panels)):
        block = plane[subspace_slab * SLAB_LENGTH : (subspace_slab + 1) * SLAB_LENGTH]
        term = lax.dot_general(
            panels[subspace_slab],
            block,
            (((0,), (0,)), ((), ())),
            precision=lax.Precision.HIGHEST,
            preferred_element_type=jnp.float32,
        )
        total = term if total is None else total + term
    return total


def per_device(
    residual_directions,
    local_field_applied,
    orbital_running_sum,
    energy_operator_running_sum,
    coefficient_store,
    slab_keepers,
    lattice_position,
):
    count = RESIDUAL_NUMBER // SLAB_LENGTH
    panels = []
    for subspace_slab in range(count):
        slab_piece = coefficient_store[
            0, subspace_slab * SLAB_LENGTH : (subspace_slab + 1) * SLAB_LENGTH
        ]
        panels.append(
            from_root(slab_piece, "band", slab_keepers[subspace_slab]).astype(jnp.float32)
        )
    outgoing = (residual_directions, local_field_applied)
    local_kinetic = kinetic_of(lattice_position)
    corr_part = lax.all_to_all(outgoing[0], "pw", split_axis=3, concat_axis=1, tiled=True)
    second_part = lax.all_to_all(outgoing[1], "pw", split_axis=3, concat_axis=1, tiled=True)
    planes_count = corr_part.shape[0]
    rows = corr_part.shape[1]
    width = corr_part.shape[3]
    corr_flat = corr_part.reshape(planes_count, rows, width)
    second_flat = second_part.reshape(planes_count, rows, width)
    hcorr_flat = local_kinetic.reshape(1, 1, width) * corr_flat + second_flat
    psi_planes = [
        rotate_plane(panels, corr_flat[plane_index]) for plane_index in range(planes_count)
    ]
    hpsi_planes = [
        rotate_plane(panels, hcorr_flat[plane_index]) for plane_index in range(planes_count)
    ]
    span = psi_planes[0].shape[0]
    psi_stack = jnp.stack(psi_planes, axis=0).reshape(planes_count, span, 1, width)
    hpsi_stack = jnp.stack(hpsi_planes, axis=0).reshape(planes_count, span, 1, width)
    psi_new = (orbital_running_sum.astype(jnp.float32) + psi_stack).astype(jnp.bfloat16)
    hpsi_new = (energy_operator_running_sum.astype(jnp.float32) + hpsi_stack).astype(jnp.bfloat16)
    return (psi_new, hpsi_new)


def solution(mesh):
    in_specs = (
        P(None, "pw", "band", None),
        P(None, "pw", "band", None),
        P(None, None, "band", "pw"),
        P(None, None, "band", "pw"),
        P("band", None, None),
        P(),
        P("band", "pw"),
    )
    out_specs = (P(None, None, "band", "pw"), P(None, None, "band", "pw"))
    return jax.shard_map(
        per_device, mesh=mesh, in_specs=in_specs, out_specs=out_specs, check_vma=False
    )
```

profile of v0, /device:TPU:6, one launch (start us, length us, event | category | flops | bytes accessed | tf_op | source)
XLA Modules:
  0.0 261.7 jit_solution(14496637142903261948)
XLA Ops:
  7.2 17.4 %copy.42 = f32[2,8,1,16384]{1,0,2,3:T(2,128)} copy(f32[2,8,1,16384]{3,2,1,0:T(1,128)} %param.7) | data formatting | bytes 2097152 | tf_op args[0]
  24.6 29.0 %reshape.42 = f32[64,1,4096]{2,1,0:T(1,128)} reshape(f32[16384,1,2,8]{3,2,1,0:T(2,128)} %bitcast.92) | data formatting | bytes 2097152
  53.5 0.0 copy-start.4
  53.5 13.3 %all-to-all-start = ((f32[64,1,4096]{2,1,0:T(1,128)}), f32[64,1,4096]{2,1,0:T(1,128)S(1)}, u32[]{:S(2)}, u32[]{:S(2)}) async-start(f32[64,1,4096]{2,1,0:T(1,128)} %reshape.42), calls=%async_computation | async-start | bytes 2097152 | tf_op jit(solution)/shard_map/all_to_all | solution.py:62
  66.9 0.0 copy-done.4
  66.9 14.6 %copy.50 = f32[2,8,1,16384]{1,0,2,3:T(2,128)} copy(f32[2,8,1,16384]{3,2,1,0:T(1,128)S(1)} %copy-done.4) | data formatting | bytes 2097152 | tf_op args[1]
  81.4 28.9 %reshape.44 = f32[64,1,4096]{2,1,0:T(1,128)} reshape(f32[16384,1,2,8]{3,2,1,0:T(2,128)} %bitcast.93) | data formatting | bytes 2097152
  110.4 0.0 copy-start.8
  110.4 0.0 all-to-all-done
  110.4 11.6 %all-to-all-start.1 = ((f32[64,1,4096]{2,1,0:T(1,128)}), f32[64,1,4096]{2,1,0:T(1,128)}, u32[]{:S(2)}, u32[]{:S(2)}) async-start(f32[64,1,4096]{2,1,0:T(1,128)} %reshape.44), calls=%async_computation.1 | async-start | bytes 2097152 | tf_op jit(solution)/shard_map/all_to_all | solution.py:63
  122.0 0.2 all-reduce.3.cloned.1.call-start
  122.2 0.0 copy-done.8
  122.3 0.6 fusion.29
  124.1 3.0 %select_bitcast_fusion = (bf16[256,2048]{1,0:T(8,128)(2,1)}, bf16[256,2048]{1,0:T(8,128)(2,1)}) fusion(bf16[1,512,2048]{2,1,0:T(8,128)(2,1)} %param.11, pred[]{:T(512)S(6)} %eq.10, pred[]{:T(512)S(6)} %eq.9), kind=kLoop, calls=%fused_computation.18 | loop fusion | flops 1048576 | bytes 4194306 | tf_op jit(solution)/shard_map/jit(_where)/select_n | solution.py:12
  127.1 0.0 copy-start.9
  127.1 0.0 all-reduce.3.cloned.1.call-update
  127.2 0.7 copy-done.9
  127.8 0.6 broadcast.42
  128.4 3.3 %reduce.1 = f32[64,4096]{1,0:T(8,128)S(1)} reduce(f32[64,1,4096]{2,1,0:T(1,128)S(1)} %all-to-all-done, f32[]{:T(128)} %broadcast.42), dimensions={1}, to_apply=%all_to_all.22.reduce_sub_computation | reduce | bytes 2097156 | tf_op jit(solution)/shard_map/all_to_all | solution.py:62
  131.7 26.7 %reshape.43 = f32[16384,1,2,8]{3,2,1,0:T(2,128)} reshape(f32[64,4096]{1,0:T(8,128)S(1)} %reduce.1) | data formatting | bytes 2097152
  158.4 17.8 %copy.56 = f32[2,8,1,64,256]{4,1,3,0,2:T(8,128)S(1)} copy(f32[2,8,1,64,256]{1,0,4,3,2:T(2,128)} %bitcast.89) | data formatting | bytes 2097152 | tf_op jit(solution)/shard_map/all_to_all | solution.py:62
  176.2 13.2 %copy.55 = f32[2,8,1,64,256]{4,3,1,0,2:T(8,128)S(1)} copy(f32[2,8,1,64,256]{1,0,4,3,2:T(2,128)} %bitcast.90) | data formatting | bytes 2097152 | tf_op jit(solution)/shard_map/all_to_all | solution.py:62
  189.4 0.0 all-to-all-done.1
  189.4 4.4 %reduce = f32[64,4096]{1,0:T(8,128)S(1)} reduce(f32[64,1,4096]{2,1,0:T(1,128)} %all-to-all-done.1, f32[]{:T(128)} %broadcast.42), dimensions={1}, to_apply=%all_to_all.25.reduce_sub_computation | reduce | bytes 2097156 | tf_op jit(solution)/shard_map/all_to_all | solution.py:63
  193.8 26.7 %reshape.45 = f32[16384,1,2,8]{3,2,1,0:T(2,128)} reshape(f32[64,4096]{1,0:T(8,128)S(1)} %reduce) | data formatting | bytes 2097152
  220.5 17.8 %copy.58 = f32[2,8,1,64,256]{4,1,3,0,2:T(8,128)S(1)} copy(f32[2,8,1,64,256]{1,0,4,3,2:T(2,128)} %bitcast.91) | data formatting | bytes 2097152 | tf_op jit(solution)/shard_map/all_to_all | solution.py:63
  238.4 0.9 fusion.28
  239.3 0.1 bitcast_add_fusion
  239.4 0.0 all-reduce.3.cloned.1.call-done
  239.4 0.0 copy-start
  239.4 2.6 fusion.10
  242.0 0.0 copy-done
  242.0 0.0 copy-start.1
  242.0 1.3 fusion.11
  243.3 0.0 copy-done.1
  243.3 1.3 fusion.4
  244.6 0.0 copy-start.5
  244.6 1.3 fusion.5
  246.0 0.0 copy-done.5
  246.0 1.3 fusion.13
  247.3 0.0 copy-start.7
  247.3 1.3 fusion.16
  248.7 0.0 copy-done.7
  248.7 0.0 copy-start.6
  248.7 1.4 fusion.6
  250.1 0.0 copy-done.6
  250.1 0.0 copy-start.2
  250.1 0.0 copy-start.3
  250.1 1.4 fusion.7
  251.5 0.2 copy-done.2
  251.7 0.6 copy-done.3
  252.3 2.5 fusion.8
  (1 shorter events, 0.0 us)
Async XLA Ops:
  53.5 13.4 %copy-start.4 = (f32[2,8,1,16384]{3,2,1,0:T(1,128)S(1)}, f32[2,8,1,16384]{3,2,1,0:T(1,128)}, u32[]{:S(2)}) copy-start(f32[2,8,1,16384]{3,2,1,0:T(1,128)} %param.8) | copy-start | bytes 3145732
  53.5 56.9 %all-to-all-start = ((f32[64,1,4096]{2,1,0:T(1,128)}), f32[64,1,4096]{2,1,0:T(1,128)S(1)}, u32[]{:S(2)}, u32[]{:S(2)}) async-start(f32[64,1,4096]{2,1,0:T(1,128)} %reshape.42), calls=%async_computation | async-start | bytes 2097152 | tf_op jit(solution)/shard_map/all_to_all | solution.py:62
  110.4 11.9 %copy-start.8 = (s32[2]{0:T(128)S(1)}, s32[2]{0:T(128)}, u32[]{:S(2)}) copy-start(s32[2]{0:T(128)} %param.12) | copy-start | bytes 28
  110.4 79.0 %all-to-all-start.1 = ((f32[64,1,4096]{2,1,0:T(1,128)}), f32[64,1,4096]{2,1,0:T(1,128)}, u32[]{:S(2)}, u32[]{:S(2)}) async-start(f32[64,1,4096]{2,1,0:T(1,128)} %reshape.44), calls=%async_computation.1 | async-start | bytes 2097152 | tf_op jit(solution)/shard_map/all_to_all | solution.py:63
  122.0 117.4 %all-reduce.3.cloned.1.call-start = ((), (), s32[]{:S(2)}) async-start(), calls=%async_computation.2 | async-start | bytes 4194304 | tf_op jit(solution)/shard_map/psum | solution.py:13
  127.1 0.7 copy-start.9
  239.4 2.6 copy-start
  242.0 1.3 copy-start.1
  244.6 1.3 copy-start.5
  247.3 1.4 copy-start.7
  248.7 1.4 copy-start.6
  250.1 1.6 copy-start.2
  250.1 2.2 copy-start.3
Sparse Core Ops, SparseCore 0:
  127.3 65.1 all-reduce.2
where the time goes:
time: 265 us; the launch traced here: 262 us
  local copies, waits for them, and re-layouts  196 us (74%)
  starting transfers between devices  25.2 us (10%)
  between operations  15.6 us (6%)
  other arithmetic  13.3 us (5%)
  matrix products  11.9 us (4%)
    unnamed x26, local copies, waits for them, and re-layouts  145 us
    all_to_all x2, local copies, waits for them, and re-layouts, per_device(): lax.all_to_all(outgoing[0], 'pw', split_axis=3, concat_axis=1, tiled=True)  31 us
    all_to_all x2, local copies, waits for them, and re-layouts, per_device(): lax.all_to_all(outgoing[1], 'pw', split_axis=3, concat_axis=1, tiled=True)  18.4 us
    all_to_all x1, starting transfers between devices, per_device(): lax.all_to_all(outgoing[0], 'pw', split_axis=3, concat_axis=1, tiled=True)  13.3 us
    dot_general x8, matrix products, rotate_plane(): lax.dot_general(panels[subspace_slab], block, (((0,), (0,)), ((), ())), p...  11.9 us
    all_to_all x1, starting transfers between devices, per_device(): lax.all_to_all(outgoing[1], 'pw', split_axis=3, concat_axis=1, tiled=True)  11.6 us
  transfers between devices with their start and end apart: 3, of which 0 were waited for; matrix products, arithmetic and copies ran while one was open for 61% of the time, Pallas kernels for 0%

commit v1 on v0

--- a/solution.py
+++ b/solution.py
@@ -6,6 +6,12 @@
 RESIDUAL_NUMBER = 512
 SLAB_LENGTH = 256
 GRID = 64
+
+
+def trade_parts(array, mesh_axis, split, join):
+    cells = jnp.split(array, lax.axis_size(mesh_axis), axis=split)
+    arrived = lax.all_to_all(jnp.stack(cells), mesh_axis, 0, 0)
+    return jnp.concatenate(arrived, axis=join)
 
 
 def from_root(value, axis, source):
@@ -59,7 +65,7 @@
         )
     outgoing = (residual_directions, local_field_applied)
     local_kinetic = kinetic_of(lattice_position)
-    corr_part = lax.all_to_all(outgoing[0], "pw", split_axis=3, concat_axis=1, tiled=True)
+    corr_part = trade_parts(outgoing[0], "pw", 3, 1)
     second_part = lax.all_to_all(outgoing[1], "pw", split_axis=3, concat_axis=1, tiled=True)
     planes_count = corr_part.shape[0]
     rows = corr_part.shape[1]

time: 265 us -> 216 us (0.82)
  the two profiles are of different devices: /device:TPU:6 before, /device:TPU:1 now
where the time goes in v1:
time: 216 us; the launch traced here: 214 us
  local copies, waits for them, and re-layouts  133 us (62%)
  starting transfers between devices  24.5 us (11%)
  waiting for transfers between devices  19.5 us (9%)
  between operations  15.6 us (7%)
  matrix products  11.7 us (5%)
  other arithmetic  9.92 us (5%)
    unnamed x82, local copies, waits for them, and re-layouts  112 us
    psum x1, waiting for transfers between devices, from_root(): return lax.psum(kept, axis)  19.4 us
    all_to_all x2, local copies, waits for them, and re-layouts, per_device(): lax.all_to_all(outgoing[1], 'pw', split_axis=3, concat_axis=1, tiled=True)  18.4 us
    all_to_all x1, starting transfers between devices, per_device(): lax.all_to_all(outgoing[1], 'pw', split_axis=3, concat_axis=1, tiled=True)  13.7 us
    dot_general x8, matrix products, rotate_plane(): lax.dot_general(panels[subspace_slab], block, (((0,), (0,)), ((), ())), p...  11.7 us
    all_to_all x1, starting transfers between devices, trade_parts(): arrived = lax.all_to_all(jnp.stack(cells), mesh_axis, 0, 0)  10.7 us
  transfers between devices with their start and end apart: 3, of which 1 were waited for; matrix products, arithmetic and copies ran while one was open for 43% of the time, Pallas kernels for 0%

profile of v1, /device:TPU:1, one launch (start us, length us, event | category | flops | bytes accessed | tf_op | source)
XLA Modules:
  0.0 214.1 jit_solution(15320392186818600661)
XLA Ops:
  7.2 17.4 %copy.289 = f32[2,8,1,16384]{1,0,2,3:T(2,128)} copy(f32[2,8,1,16384]{3,2,1,0:T(1,128)} %param.8) | data formatting | bytes 2097152 | tf_op args[1]
  24.5 29.0 %reshape.41 = f32[64,1,4096]{2,1,0:T(1,128)} reshape(f32[16384,1,2,8]{3,2,1,0:T(2,128)} %bitcast.344) | data formatting | bytes 2097152
  53.5 13.7 %all-to-all-start.1 = ((f32[64,1,4096]{2,1,0:T(1,128)}), f32[64,1,4096]{2,1,0:T(1,128)S(1)}, u32[]{:S(2)}, u32[]{:S(2)}) async-start(f32[64,1,4096]{2,1,0:T(1,128)} %reshape.41), calls=%async_computation.1 | async-start | bytes 2097152 | tf_op jit(solution)/shard_map/all_to_all | solution.py:69
  68.2 0.6 constant_dynamic-update-slice_fusion.63
  69.4 0.6 constant_dynamic-update-slice_fusion.61
  70.0 0.6 constant_dynamic-update-slice_fusion.60
  70.6 0.6 constant_dynamic-update-slice_fusion.59
  71.2 0.6 constant_dynamic-update-slice_fusion.58
  71.8 0.6 constant_dynamic-update-slice_fusion.57
  72.4 0.6 constant_dynamic-update-slice_fusion.56
  73.0 0.6 constant_dynamic-update-slice_fusion.55
  73.6 0.6 constant_dynamic-update-slice_fusion.54
  74.8 0.6 constant_dynamic-update-slice_fusion.52
  75.4 0.6 constant_dynamic-update-slice_fusion.51
  76.6 0.6 constant_dynamic-update-slice_fusion.49
  77.2 0.6 constant_dynamic-update-slice_fusion.48
  78.4 0.6 constant_dynamic-update-slice_fusion.46
  79.0 0.6 constant_dynamic-update-slice_fusion.45
  79.6 0.6 constant_dynamic-update-slice_fusion.44
  80.2 0.6 constant_dynamic-update-slice_fusion.43
  80.8 0.6 constant_dynamic-update-slice_fusion.42
  82.0 0.6 constant_dynamic-update-slice_fusion.40
  83.2 0.6 constant_dynamic-update-slice_fusion.38
  84.4 0.6 constant_dynamic-update-slice_fusion.36
  85.0 0.6 constant_dynamic-update-slice_fusion.35
  86.2 0.6 constant_dynamic-update-slice_fusion.33
  86.8 0.6 constant_dynamic-update-slice_fusion.32
  88.0 0.6 constant_dynamic-update-slice_fusion.30
  88.6 0.6 constant_dynamic-update-slice_fusion.29
  89.2 0.6 constant_dynamic-update-slice_fusion.28
  91.0 0.6 constant_dynamic-update-slice_fusion.25
  91.6 0.6 constant_dynamic-update-slice_fusion.24
  92.2 0.6 constant_dynamic-update-slice_fusion.23
  92.8 0.6 constant_dynamic-update-slice_fusion.22
  94.6 0.6 constant_dynamic-update-slice_fusion.19
  95.2 0.6 constant_dynamic-update-slice_fusion.18
  96.4 0.6 constant_dynamic-update-slice_fusion.16
  97.0 0.6 constant_dynamic-update-slice_fusion.15
  97.6 0.6 constant_dynamic-update-slice_fusion.14
  100.6 0.6 constant_dynamic-update-slice_fusion.9
  103.1 0.6 constant_dynamic-update-slice_fusion.8
  103.8 0.6 constant_dynamic-update-slice_fusion.7
  105.6 0.6 constant_dynamic-update-slice_fusion.4
  106.2 0.6 constant_dynamic-update-slice_fusion.3
  106.8 0.6 constant_dynamic-update-slice_fusion.2
  108.0 0.6 constant_dynamic-update-slice_fusion
  108.6 10.7 %all-to-all-start = ((f32[64,2,8,1,256]{4,2,1,3,0:T(8,128)}), f32[64,2,8,1,256]{4,2,1,3,0:T(8,128)S(1)}, u32[]{:S(2)}, u32[]{:S(2)}) async-start(f32[64,2,8,1,256]{4,2,1,3,0:T(8,128)} %constant_dynamic-update-slice_fusion), calls=%async_computation | async-start | bytes 2097152 | tf_op jit(solution)/shard_map/all_to_all | solution.py:13
  119.3 3.0 %select_bitcast_fusion = (bf16[256,2048]{1,0:T(8,128)(2,1)}, bf16[256,2048]{1,0:T(8,128)(2,1)}) fusion(bf16[1,512,2048]{2,1,0:T(8,128)(2,1)} %param.11, pred[]{:T(512)S(6)} %eq.10, pred[]{:T(512)S(6)} %eq.9), kind=kLoop, calls=%fused_computation.18 | loop fusion | flops 1048576 | bytes 4194306 | tf_op jit(solution)/shard_map/jit(_where)/select_n | solution.py:18
  122.4 0.7 copy-done.7
  123.6 3.3 %reduce = f32[64,4096]{1,0:T(8,128)S(1)} reduce(f32[64,1,4096]{2,1,0:T(1,128)S(1)} %all-to-all-done.1, f32[]{:T(128)} %broadcast.42), dimensions={1}, to_apply=%all_to_all.15.reduce_sub_computation | reduce | bytes 2097156 | tf_op jit(solution)/shard_map/all_to_all | solution.py:69
  127.0 26.7 %reshape.42 = f32[16384,1,2,8]{3,2,1,0:T(2,128)} reshape(f32[64,4096]{1,0:T(8,128)S(1)} %reduce) | data formatting | bytes 2097152
  153.6 17.8 %copy.295 = f32[2,8,1,64,256]{4,1,3,0,2:T(8,128)S(1)} copy(f32[2,8,1,64,256]{1,0,4,3,2:T(2,128)} %bitcast.343) | data formatting | bytes 2097152 | tf_op jit(solution)/shard_map/all_to_all | solution.py:69
  171.5 1.1 bitcast_add_fusion
  172.7 19.4 %all-reduce.3.cloned.1.call-done = (bf16[256,2048]{1,0:T(8,128)(2,1)}, bf16[256,2048]{1,0:T(8,128)(2,1)}) async-done(((bf16[256,2048]{1,0:T(8,128)(2,1)}, bf16[256,2048]{1,0:T(8,128)(2,1)}), (bf16[256,2048]{1,0:T(8,128)(2,1)}, bf16[256,2048]{1,0:T(8,128)(2,1)})) %all-reduce.3.cloned.1.call-update) | async-done | bytes 2097168 | tf_op jit(solution)/shard_map/psum | solution.py:19
  192.1 2.6 %fusion.10 = f32[2048,256]{1,0:T(8,128)S(1)} fusion(bf16[256,2048]{1,0:T(8,128)(2,1)} %get-tuple-element.12, f32[2,512,256]{2,1,0:T(8,128)} %bitcast_add_fusion), kind=kOutput, calls=%fused_computation.23 | convolution fusion | flops 1610612736 | bytes 3407872 | tf_op jit(solution)/shard_map/dot_general | solution.py:37
  194.7 1.3 fusion.11
  196.0 1.3 fusion.12
  197.3 1.3 fusion.13
  198.5 1.3 fusion.4
  199.9 1.3 fusion.5
  201.2 1.3 fusion.6
  202.6 1.3 fusion.7
  204.1 0.6 copy-done.4
  204.8 2.5 %fusion.8 = (bf16[2,2048,1,256]{3,1,2,0:T(8,128)(2,1)}, bf16[2,2048,1,256]{3,1,2,0:T(8,128)(2,1)}) fusion(f32[1,2048,256]{2,1,0:T(8,128)S(1)} %fusion.4, f32[1,2048,256]{2,1,0:T(8,128)S(1)} %fusion.5, bf16[2,2048,1,256]{3,1,2,0:T(8,128)(2,1)S(1)} %copy-done.3, f32[1,2048,256]{2,1,0:T(8,128)S(1)} %fusion.6, f32[1,2048,256]{2,1,0:T(8,128)S(1)} %fusion.7, ...), kind=kLoop, calls=%fused_computation.14 | loop fusion | flops 8388608 | bytes 16777216
  (47 shorter events, 15.1 us)
Async XLA Ops:
  53.5 13.7 %copy-start.5 = (f32[2,8,1,16384]{3,2,1,0:T(1,128)S(1)}, f32[2,8,1,16384]{3,2,1,0:T(1,128)}, u32[]{:S(2)}) copy-start(f32[2,8,1,16384]{3,2,1,0:T(1,128)} %param.7) | copy-start | bytes 3145732
  53.5 55.1 %all-to-all-start.1 = ((f32[64,1,4096]{2,1,0:T(1,128)}), f32[64,1,4096]{2,1,0:T(1,128)S(1)}, u32[]{:S(2)}, u32[]{:S(2)}) async-start(f32[64,1,4096]{2,1,0:T(1,128)} %reshape.41), calls=%async_computation.1 | async-start | bytes 2097152 | tf_op jit(solution)/shard_map/all_to_all | solution.py:69
  67.2 34.0 %copy-start.6 = (s32[2]{0:T(128)S(1)}, s32[2]{0:T(128)}, u32[]{:S(2)}) copy-start(s32[2]{0:T(128)} %param.12) | copy-start | bytes 28
  108.6 62.9 %all-to-all-start = ((f32[64,2,8,1,256]{4,2,1,3,0:T(8,128)}), f32[64,2,8,1,256]{4,2,1,3,0:T(8,128)S(1)}, u32[]{:S(2)}, u32[]{:S(2)}) async-start(f32[64,2,8,1,256]{4,2,1,3,0:T(8,128)} %constant_dynamic-update-slice_fusion), calls=%async_computation | async-start | bytes 2097152 | tf_op jit(solution)/shard_map/all_to_all | solution.py:13
  119.3 72.8 %all-reduce.3.cloned.1.call-start = ((), (), s32[]{:S(2)}) async-start(), calls=%async_computation.2 | async-start | bytes 4194304 | tf_op jit(solution)/shard_map/psum | solution.py:19
  122.3 0.7 copy-start.7
  172.7 22.1 %copy-start.2 = (f32[2,512,256]{2,1,0:T(8,128)S(1)}, f32[2,512,256]{2,1,0:T(8,128)}, u32[]{:S(2)}) copy-start(f32[2,512,256]{2,1,0:T(8,128)} %bitcast_add_fusion) | copy-start | bytes 3145732
  192.1 2.6 %copy-start = (bf16[256,2048]{1,0:T(8,128)(2,1)S(1)}, bf16[256,2048]{1,0:T(8,128)(2,1)}, u32[]{:S(2)}) copy-start(bf16[256,2048]{1,0:T(8,128)(2,1)} %get-tuple-element.12) | copy-start | bytes 3145732
  197.3 1.3 copy-start.1
  202.5 1.6 copy-start.3
  202.5 2.2 %copy-start.4 = (bf16[2,2048,1,256]{3,1,2,0:T(8,128)(2,1)S(1)}, bf16[2,2048,1,256]{3,1,2,0:T(8,128)(2,1)}, u32[]{:S(2)}) copy-start(bf16[2,2048,1,256]{3,1,2,0:T(8,128)(2,1)} %param.9) | copy-start | bytes 6291460
Sparse Core Ops, SparseCore 0:
  123.4 68.6 all-reduce.2
